TPU v7x, 256 devices: a whole 4x4x8 slice. The times are simulated.
256 devices in a mesh: shard: 16 (over x, z_hi, core), rep: 16 (over y, z_lo).
Axes of the slice: x: 4, y: 4, z: 8 (z_hi: 2, z_lo: 4; z = z_hi * 4 + z_lo), core: 2. Of those that a mesh axis runs over, the one named last changes fastest.
Arguments:
- grads: bfloat16 [16, 16, 2097152], P('shard', 'rep'), may hold values from -5000 to 5000
- momentum_codes: int32 [2097152], P(('shard', 'rep')), may hold values from -127 to 127
- variance_codes: int32 [2097152], P(('shard', 'rep')), may hold values from 16 to 255
- momentum_scale: float32 [1280], P(('shard', 'rep')), may hold values from 0.5 to 4, as said below
- variance_scale: float32 [1280], P(('shard', 'rep')), may hold values from 1 to 4, as said below
- master: float32 [2097152], P(('shard', 'rep')), may hold values from -2.5 to 2.5
- step: int32 [1], replicated, may hold values from 1 to 19
Outputs:
- new_master: float32 [2097152], P(('shard', 'rep'))
- weights: bfloat16 [2097152], P('shard')
- update: float32 [2097152], P(('shard', 'rep'))
- momentum_norm: float32 [2097152], P(('shard', 'rep'))
- variance_norm: float32 [2097152], P(('shard', 'rep'))
- momentum_absmax: float32 [1280], P(('shard', 'rep'))
- variance_absmax: float32 [1280], P(('shard', 'rep'))
Inputs may be any that keep to these rules, and one draw needn't show every extreme that they name: `momentum_scale`: A block touched by two neighbouring devices has the same value in both devices' slots. `variance_scale`: A block touched by two neighbouring devices has the same value in both devices' slots.
All inputs are finite; a program needn't handle non-finite values.
Results may differ from a plain program's by a relative error of at most 0.0004.
Values may be sent and summed in bfloat16 or wider, within the bound.
A program may use at most 64 MiB of HBM per device.

v0:
```python
import jax
import jax.numpy as jnp
from jax import lax
from jax.sharding import PartitionSpec as P

BLOCK = 2048


def extended(block, sides, width):
    for axis, dim in sides:
        count = lax.axis_size(axis)
        forward = [(i, i + 1) for i in range(count - 1)]
        backward = [(target, source) for source, target in forward]
        low = lax.ppermute(
            lax.slice_in_dim(block, block.shape[dim] - width, None, axis=dim), axis, forward
        )
        high = lax.ppermute(lax.slice_in_dim(block, 0, width, axis=dim), axis, backward)
        block = jnp.concatenate([low, block, high], axis=dim)
    return block


def on_device(grads, momentum_codes, variance_codes, momentum_scale, variance_scale, master, step):
    own_len = master.shape[0]
    slot_count = momentum_scale.shape[0]
    block_len = BLOCK
    half_len = block_len // 2
    shard_count = lax.axis_size("shard")
    rep_count = lax.axis_size("rep")
    grad_terms = grads.reshape(-1).astype(jnp.float32)
    partial_sum = lax.psum_scatter(grad_terms, "shard", scatter_dimension=0, tiled=True)
    gsum = lax.psum_scatter(partial_sum, "rep", scatter_dimension=0, tiled=True)
    norm_sq = lax.psum(jnp.sum(gsum * gsum), ("shard", "rep"))
    total_params = own_len * shard_count * rep_count
    clip_factor = jnp.minimum(1.0, float(total_params) ** 0.5 / (jnp.sqrt(norm_sq) + 1e-06))
    scaled = gsum * clip_factor

    def spread(scale_table):
        return jnp.repeat(scale_table, block_len)[half_len : half_len + own_len]

    m_old = momentum_codes.astype(jnp.float32) / 127.0 * spread(momentum_scale)
    v_old = variance_codes.astype(jnp.float32) / 255.0 * spread(variance_scale)
    momentum = 0.9 * m_old + 0.1 * scaled
    variance = 0.95 * v_old + 0.05 * scaled * scaled
    count = step[0].astype(jnp.float32)
    first_fix = 1.0 - jnp.power(jnp.float32(0.9), count)
    second_fix = 1.0 - jnp.power(jnp.float32(0.95), count)
    update = momentum / first_fix / (jnp.sqrt(variance / second_fix) + 1e-08)
    new_master = master * (1.0 - 0.0001 * 0.1) - 0.0001 * update
    weights = lax.all_gather(new_master.astype(jnp.bfloat16), "rep", axis=0, tiled=True)

    def slot_max(values):
        padded = jnp.pad(jnp.abs(values), (half_len, half_len))
        return jnp.max(padded.reshape(slot_count, block_len), axis=1)

    m_table = slot_max(momentum)
    v_table = slot_max(variance)
    own_edge = jnp.stack(
        [jnp.stack([m_table[0], v_table[0]]), jnp.stack([m_table[-1], v_table[-1]])]
    )
    rim_vals = extended(own_edge, ((("shard", "rep"), 0),), 1)
    m_table = m_table.at[0].max(rim_vals[0, 0]).at[-1].max(rim_vals[3, 0])
    v_table = v_table.at[0].max(rim_vals[0, 1]).at[-1].max(rim_vals[3, 1])
    momentum_norm = momentum / (spread(m_table) + 1e-06)
    variance_norm = variance / (spread(v_table) + 1e-06)
    return (new_master, weights, update, momentum_norm, variance_norm, m_table, v_table)


def solution(mesh):
    in_specs = (
        P("shard", "rep", None),
        P(("shard", "rep")),
        P(("shard", "rep")),
        P(("shard", "rep")),
        P(("shard", "rep")),
        P(("shard", "rep")),
        P(),
    )
    out_specs = (
        P(("shard", "rep")),
        P("shard"),
        P(("shard", "rep")),
        P(("shard", "rep")),
        P(("shard", "rep")),
        P(("shard", "rep")),
        P(("shard", "rep")),
    )
    return jax.shard_map(
        on_device, mesh=mesh, in_specs=in_specs, out_specs=out_specs, check_vma=False
    )
```

profile of v0, /device:TPU:2, one launch (start us, length us, event | category | flops | bytes accessed | tf_op | source)
XLA Modules:
  0.0 717.0 jit_solution(4956482309576053359)
XLA Ops:
  7.2 10.8 %convert_element_type.28 = f32[1,1,2097152]{2,1,0:T(1,128)} convert(bf16[1,1,2097152]{2,1,0:T(2,128)(2,1)} %param.15) | non-fusion elementwise | flops 2097152 | bytes 12582912 | tf_op jit(solution)/shard_map/convert_element_type | solution.py:29
  20.0 379.7 %all-reduce.7.cloned.1.call-done = f32[2097152]{0:T(1024)} async-done(((f32[2097152]{0:T(1024)}), f32[2097152]{0:T(1024)}) %all-reduce.7.cloned.1.call-update) | async-done | bytes 8388624
  399.7 1.9 dynamic-slice.25
  401.7 0.6 dynamic-slice.26
  403.8 161.5 %all-reduce.9.cloned.1.call-done = f32[131072]{0:T(1024)} async-done(((f32[131072]{0:T(1024)}), f32[131072]{0:T(1024)}) %all-reduce.9.cloned.1.call-update) | async-done | bytes 524304
  565.3 1.4 multiply_reduce_fusion
  566.7 75.3 %psum.7 = f32[]{:T(128)} all-reduce(f32[]{:T(128)} %multiply_reduce_fusion), channel_id=1, replica_groups=mesh['shard'=16,'rep'=16] {'shard','rep'}, use_global_device_ids=true, to_apply=%region_3.0 | all-reduce | flops 1 | bytes 8 | tf_op jit(solution)/shard_map/psum | solution.py:32
  642.7 0.8 fusion.6
  643.7 0.6 slice.84
  644.4 0.6 slice.83
  645.0 1.4 maximum_bitcast_fusion
  646.4 1.9 collective-permute-start
  648.3 7.2 %collective-permute-done = f32[1,2]{1,0:T(1,128)S(1)} collective-permute-done((f32[1,2]{1,0:T(1,128)S(1)}, f32[1,2]{1,0:T(1,128)S(1)}, u32[]{:S(2)}, u32[]{:S(2)}) %collective-permute-start) | collective-permute-done | bytes 40 | tf_op jit(solution)/shard_map/ppermute | solution.py:14
  655.5 0.6 fusion.12
  656.0 1.8 constant_dynamic-update-slice_fusion.2
  657.9 1.4 maximum_bitcast_fusion.1
  659.2 1.9 collective-permute-start.1
  661.1 3.5 collective-permute-done.1
  664.7 0.6 fusion.11
  665.3 0.8 constant_dynamic-update-slice_fusion
  666.1 0.8 constant_dynamic-update-slice_fusion.1
  667.1 0.7 fusion.10
  667.7 41.7 %all_gather.3 = bf16[131072]{0:T(1024)(128)(2,1)S(1)} all-gather(bf16[8192]{0:T(1024)(128)(2,1)S(1)} %get-tuple-element.59), channel_id=1, replica_groups=mesh['shard'=16,'rep'=16] {'rep'}, dimensions={0}, use_global_device_ids=true | all-gather | bytes 278528 | tf_op jit(solution)/shard_map/all_gather | solution.py:49
  709.5 0.7 copy.22
  (37 shorter events, 1.9 us)
Async XLA Ops:
  7.2 392.5 %all-reduce.7.cloned.1.call-start = ((), (), s32[]{:S(2)}) async-start(), calls=%async_computation | async-start | bytes 16777216
  18.1 0.7 copy-start.8
  18.1 383.6 %copy-start.7 = (u32[256]{0:T(256)S(1)}, u32[256]{0:T(256)}, u32[]{:S(2)}) copy-start(u32[256]{0:T(256)} %constant.134) | copy-start | bytes 3076
  18.1 384.2 %copy-start.5 = (f32[5]{0:T(128)S(1)}, f32[5]{0:T(128)}, u32[]{:S(2)}) copy-start(f32[5]{0:T(128)} %param.19) | copy-start | bytes 64
  18.1 384.3 %copy-start.6 = (f32[5]{0:T(128)S(1)}, f32[5]{0:T(128)}, u32[]{:S(2)}) copy-start(f32[5]{0:T(128)} %param.18) | copy-start | bytes 64
  18.1 624.6 %copy-start = (s32[8192]{0:T(1024)S(1)}, s32[8192]{0:T(1024)}, u32[]{:S(2)}) copy-start(s32[8192]{0:T(1024)} %param.17) | copy-start | bytes 98308
  18.1 624.6 %copy-start.1 = (s32[8192]{0:T(1024)S(1)}, s32[8192]{0:T(1024)}, u32[]{:S(2)}) copy-start(s32[8192]{0:T(1024)} %param.16) | copy-start | bytes 98308
  18.1 648.9 %copy-start.2 = (f32[8192]{0:T(1024)S(1)}, f32[8192]{0:T(1024)}, u32[]{:S(2)}) copy-start(f32[8192]{0:T(1024)} %param.20) | copy-start | bytes 98308
  18.2 547.1 %all-reduce.9.cloned.1.call-start = ((), (), s32[]{:S(2)}) async-start(), calls=%async_computation.1 | async-start | bytes 1048576
  646.4 9.1 %collective-permute-start = (f32[1,2]{1,0:T(1,128)S(1)}, f32[1,2]{1,0:T(1,128)S(1)}, u32[]{:S(2)}, u32[]{:S(2)}) collective-permute-start(f32[1,2]{1,0:T(1,128)S(1)} %maximum_bitcast_fusion), channel_id=1, source_target_pairs={{0,1},{1,2},{2,3},{3,4},{4,5},{5,6},{6,7},{7,8},{8,9},{9,10},{10,1... | collective-permute-start | bytes 32 | tf_op jit(solution)/shard_map/ppermute | solution.py:14
  659.2 5.5 collective-permute-start.1
  666.1 44.2 %copy-start.3 = (f32[5]{0:T(128)}, f32[5]{0:T(128)S(1)}, u32[]{:S(2)}) copy-start(f32[5]{0:T(128)S(1)} %constant_dynamic-update-slice_fusion) | copy-start | bytes 64
  666.9 43.3 %copy-start.4 = (f32[5]{0:T(128)}, f32[5]{0:T(128)S(1)}, u32[]{:S(2)}) copy-start(f32[5]{0:T(128)S(1)} %constant_dynamic-update-slice_fusion.1) | copy-start | bytes 64
Sparse Core Ops, SparseCore 0:
  18.3 381.3 all-reduce.6
  402.3 162.9 all-reduce.8
where the time goes:
time: 718 us; the launch traced here: 717 us
  waiting for transfers between devices  552 us (77%)
  blocking collectives  117 us (16%)
  other arithmetic  20.1 us (3%)
  between operations  17 us (2%)
    unnamed x4, waiting for transfers between devices  541 us
    psum x1, blocking collectives, on_device(): norm_sq = lax.psum(jnp.sum(gsum * gsum), ('shard', 'rep'))  75.3 us
    all_gather x1, blocking collectives, on_device(): lax.all_gather(new_master.astype(jnp.bfloat16), 'rep', axis=0, tiled=True)  41.7 us
  transfers between devices with their start and end apart: 4, of which 4 were waited for; matrix products, arithmetic and copies ran while one was open for 0% of the time, Pallas kernels for 0%

commit v1 on v0

v1 whole, which is shorter than its diff:
```python
import math

import jax
import jax.numpy as jnp
from jax import lax
from jax.experimental import pallas as pl
from jax.experimental.pallas import tpu as pltpu
from jax.sharding import PartitionSpec as P

MESH = pl.DeviceIdType.MESH
F32 = jnp.float32
BF16 = jnp.bfloat16
OWN = 8192
ROWS = 64
PIECE = 4 * OWN
CORE_RUN = 4 * PIECE
HALF = 8 * CORE_RUN
RA, RB, RC = 24, 24, 16
SLOT_ROWS = ((0, 8), (8, 24), (24, 40), (40, 56), (56, 64))


def mod(v, n):
    return lax.rem(v + 4 * n, n)


class Copies:
    def __init__(self):
        self.sent = []

    def start(self, copy):
        copy.start()
        self.sent.append(copy)

    def finish(self):
        for copy in self.sent:
            copy.wait_send()


class Ring:
    def __init__(self, out, pos, n, work, land, send, recv, peer):
        self.out, self.pos, self.n = out, pos, n
        self.work, self.land, self.send, self.recv, self.peer = work, land, send, recv, peer
        self.index = {}
        for s, h in ((1, 0), (-1, 1), (1, 1), (-1, 0)):
            for k in range(1, self.hops(s, h) + 1):
                self.index[s, h, k] = len(self.index)

    def hops(self, s, h):
        return self.n // 2 if (s == 1) == (h == 0) else self.n // 2 - 1

    def at(self, offset):
        return mod(self.pos + offset, self.n)

    def copy(self, s, h, k):
        i = self.index[s, h, k]
        return pltpu.make_async_remote_copy(
            src_ref=self.work.at[self.at(s * (self.hops(s, h) - k + 1)), h],
            dst_ref=self.land.at[i],
            send_sem=self.send.at[i],
            recv_sem=self.recv.at[i],
            device_id=self.peer(s),
            device_id_type=MESH,
        )

    def start(self, s, h, k=1):
        self.out.start(self.copy(s, h, k))

    def step(self, s, h, k):
        self.copy(s, h, k).wait_recv()
        hops = self.hops(s, h)
        if k < hops:
            dest = self.at(s * (hops - k))
            self.work[dest, h] = self.work[dest, h] + self.land[self.index[s, h, k]]
            self.start(s, h, k + 1)

    def total(self, h):
        t = self.work[self.pos, h]
        for s in (1, -1):
            t = t + self.land[self.index[s, h, self.hops(s, h)]]
        return t


def kernel(
    g_ref, mc_ref, vc_ref, ms_ref, vs_ref, ma_ref, st_ref,
    nm_ref, wt_ref, up_ref, mn_ref, vn_ref, tb_ref,
    own, par, wa, wb, wc, la, lb, lc, sa, sb, sc, la2, lb2, ta, tb2, qa, qb, qc,
    nv, nq, nv2, nq2, ex, fx, wg,
    own_sem, par_s, par_r, a_s, a_r, b_s, b_r, c_s, c_r, a2_s, a2_r, b2_s, b2_r,
    qa_s, qa_r, qb_s, qb_r, qc_s, qc_r, n_s, n_r, n2_s, n2_r, e_s, e_r, w_s, w_r,
):
    shard = lax.axis_index("shard")
    rep = lax.axis_index("rep")
    x, zh, c = shard // 4, (shard // 2) % 2, shard % 2
    y, zl = rep // 4, rep % 4
    z = zh * 4 + zl

    def dev(xx, yy, zz, cc):
        xx, yy, zz, cc = mod(xx, 4), mod(yy, 4), mod(zz, 8), mod(cc, 2)
        return (xx * 4 + (zz // 4) * 2 + cc, yy * 4 + zz % 4)

    out = Copies()

    def remote(src, dst, send, recv, device):
        return pltpu.make_async_remote_copy(
            src_ref=src, dst_ref=dst, send_sem=send, recv_sem=recv, device_id=device, device_id_type=MESH
        )

    barrier = pltpu.get_barrier_semaphore()
    near = [dev(x, y, z, c + 1)]
    for s in (1, -1):
        near += [dev(x + s, y, z, c), dev(x, y + s, z, c), dev(x, y, z + s, c)]
    for device in near:
        pl.semaphore_signal(barrier, inc=1, device_id=device, device_id_type=MESH)

    groups = (
        [(2, d, e) for d in (1, 0) for e in range(4)],
        [(d, e, 2) for d in (1, 3, 0) for e in (1, 0)],
        [(d, 1, e) for d in (1, 3, 0) for e in (1, 3, 0)],
        [(d, 0, e) for d in (1, 3, 0) for e in (1, 3, 0)],
    )

    def piece_of(rel):
        return (mod(x + rel[0], 4) * 2 + mod(zh + rel[1], 2)) * 4 + mod(y + rel[2], 4)

    def window(ref, start):
        return ref.at[:, :, pl.ds(pl.multiple_of(start, PIECE), PIECE)]

    def start_of(piece, core):
        return (piece // 4) * (2 * CORE_RUN) + core * CORE_RUN + (piece % 4) * PIECE

    def local_piece(rel):
        p = piece_of(rel)
        return pltpu.make_async_copy(window(g_ref, start_of(p, c)), window(own, p * PIECE), own_sem.at[p])

    def partner_piece(rel):
        p = piece_of(rel)
        return remote(
            window(g_ref, start_of(p, 1 - c)), window(par, p * PIECE), par_s.at[p], par_r.at[p], dev(x, y, z, c + 1)
        )

    for group in groups:
        for rel in group:
            local_piece(rel).start()
    pl.semaphore_wait(barrier, len(near))
    for group in groups:
        for rel in group:
            out.start(partner_piece(rel))

    def arrive(group):
        for rel in group:
            local_piece(rel).wait()
            partner_piece(rel).wait_recv()

    def pair(block, first, rows):
        at = pl.ds(pl.multiple_of(block * OWN + first * 128, 1024), rows * 128)
        return own[0, 0, at].reshape(rows, 128).astype(F32) + par[0, 0, at].reshape(rows, 128).astype(F32)

    def sum_a(dx, h):
        xx = mod(x + dx, 4)

        def body(j, carry):
            base = ((xx * 2 + j % 2) * 4 + (h * 2 + j // 2)) * 4
            for i in range(4):
                wa[xx, h, j * 4 + i] = pair(base + i, 0, RA)
            return carry

        lax.fori_loop(0, 4, body, 0)

    def sum_b(dy, h):
        yy = mod(y + dy, 4)

        def body(j, carry):
            base = (((h * 2 + j // 2) * 2 + j % 2) * 4 + yy) * 4
            for i in range(4):
                wb[yy, h, j * 4 + i] = pair(base + i, RA, RB)
            return carry

        lax.fori_loop(0, 4, body, 0)

    def sum_c(dz, h):
        zz = mod(z + dz, 8)

        def body(j, carry):
            base = (((h * 2 + j) * 2 + zz // 4) * 4) * 4 + zz % 4
            for i in range(4):
                wc[zz, h, j * 4 + i] = pair(base + 4 * i, RA + RB, RC)
            return carry

        lax.fori_loop(0, 2, body, 0)

    a1 = Ring(out, x, 4, wa, la, a_s, a_r, lambda s: dev(x + s, y, z, c))
    b1 = Ring(out, y, 4, wb, lb, b_s, b_r, lambda s: dev(x, y + s, z, c))
    c1 = Ring(out, z, 8, wc, lc, c_s, c_r, lambda s: dev(x, y, z + s, c))
    a2 = Ring(out, y, 4, sa, la2, a2_s, a2_r, lambda s: dev(x, y + s, z, c))
    b2 = Ring(out, x, 4, sb, lb2, b2_s, b2_r, lambda s: dev(x + s, y, z, c))

    arrive(groups[0])
    sum_a(2, 0)
    a1.start(1, 0)
    sum_a(2, 1)
    a1.start(-1, 1)
    arrive(groups[1])
    sum_b(2, 0)
    b1.start(1, 0)
    sum_b(2, 1)
    b1.start(-1, 1)
    arrive(groups[2])
    sum_c(4, 0)
    c1.start(1, 0)
    sum_c(4, 1)
    c1.start(-1, 1)
    arrive(groups[3])
    sum_c(3, 1)
    c1.start(1, 1)
    sum_c(-3, 0)
    c1.start(-1, 0)
    sum_a(1, 1)
    a1.start(1, 1)
    sum_a(-1, 0)
    a1.start(-1, 0)
    sum_b(1, 1)
    b1.start(1, 1)
    sum_b(-1, 0)
    b1.start(-1, 0)
    sum_c(3, 0)
    sum_c(-3, 1)
    sum_a(1, 0)
    sum_a(-1, 1)
    sum_b(1, 0)
    sum_b(-1, 1)
    for h in (0, 1):
        sum_c(2, h)
        sum_c(-2, h)
    for h in (0, 1):
        sum_c(1, h)
        sum_c(-1, h)
    for h in (0, 1):
        sum_a(0, h)
        sum_b(0, h)
        sum_c(0, h)

    def long_step(ring, k):
        ring.step(1, 0, k)
        ring.step(-1, 1, k)

    def short_step(ring, k):
        ring.step(1, 1, k)
        ring.step(-1, 0, k)

    def begin(ring):
        for s, h in ((1, 0), (-1, 1), (1, 1), (-1, 0)):
            ring.start(s, h)

    steps = st_ref[0]
    first_pow = jnp.ones((8, 128), F32)
    second_pow = jnp.ones((8, 128), F32)
    taken = jnp.full((8, 128), steps, jnp.int32)
    for i in range(19):
        first_pow = jnp.where(taken > i, first_pow * 0.9, first_pow)
        second_pow = jnp.where(taken > i, second_pow * 0.95, second_pow)
    first_fix = (1.0 - first_pow)[0:1]
    second_fix = (1.0 - second_pow)[0:1]

    def spread(scale_ref):
        return jnp.concatenate([jnp.full((b - a, 128), scale_ref[i], F32) for i, (a, b) in enumerate(SLOT_ROWS)], axis=0)

    long_step(c1, 1)
    long_step(a1, 1)
    short_step(c1, 1)
    long_step(b1, 1)
    long_step(c1, 2)
    short_step(c1, 2)
    short_step(a1, 1)
    long_step(a1, 2)
    for h in (0, 1):
        t = a1.total(h)
        for i in range(2):
            for j in range(2):
                sa[h * 2 + i, j] = t[i * 8 + j * 4 : i * 8 + j * 4 + 4]
    begin(a2)
    long_step(c1, 3)
    short_step(b1, 1)
    long_step(b1, 2)
    for h in (0, 1):
        t = b1.total(h)
        for i in range(2):
            for j in range(2):
                sb[h * 2 + i, j] = t[i * 8 + j * 4 : i * 8 + j * 4 + 4]
    begin(b2)
    long_step(a2, 1)
    short_step(c1, 3)
    long_step(c1, 4)
    for h in (0, 1):
        t = c1.total(h)
        for i in range(2):
            sc[h * 2 + i] = t[i * 4 : i * 4 + 4]
    plane = [(i, j) for i in range(4) for j in range(4) if i or j]

    def plane_copy(i):
        dx, dy = plane[i]
        return remote(
            sc.at[mod(x + dx, 4), mod(y + dy, 4)], qc.at[i], qc_s.at[i], qc_r.at[i], dev(x + dx, y + dy, z, c)
        )

    for i in range(len(plane)):
        out.start(plane_copy(i))
    long_step(b2, 1)
    short_step(a2, 1)
    long_step(a2, 2)
    for h in (0, 1):
        ta[h * 4 : h * 4 + 4] = a2.total(h)

    def z_copy(src, dst, send, recv, i):
        return remote(src.at[mod(z + i + 1, 8)], dst.at[i], send.at[i], recv.at[i], dev(x, y, z + i + 1, c))

    for i in range(7):
        out.start(z_copy(ta, qa, qa_s, qa_r, i))
    short_step(b2, 1)
    long_step(b2, 2)
    for h in (0, 1):
        tb2[h * 4 : h * 4 + 4] = b2.total(h)
    for i in range(7):
        out.start(z_copy(tb2, qb, qb_s, qb_r, i))

    m_base = 0.9 * (mc_ref[...].astype(F32) / 127.0 * spread(ms_ref))
    v_base = 0.95 * (vc_ref[...].astype(F32) / 255.0 * spread(vs_ref))
    kept = ma_ref[...] * (1.0 - 0.0001 * 0.1)

    gc = sc[x, y]
    for i in range(len(plane)):
        plane_copy(i).wait_recv()
        gc = gc + qc[i]
    ga = ta[z]
    for i in range(7):
        z_copy(ta, qa, qa_s, qa_r, i).wait_recv()
        ga = ga + qa[i]
    gb = tb2[z]
    for i in range(7):
        z_copy(tb2, qb, qb_s, qb_r, i).wait_recv()
        gb = gb + qb[i]
    gsum = jnp.concatenate([ga, gb, gc], axis=0)

    nv[...] = jnp.sum(gsum * gsum, axis=0, keepdims=True)
    around = [(i, j, k) for i in range(4) for j in range(4) for k in range(2) if i or j or k]

    def norm_copy(i):
        dx, dy, dc = around[i]
        return remote(nv, nq.at[i], n_s.at[i], n_r.at[i], dev(x + dx, y + dy, z, c + dc))

    for i in range(len(around)):
        out.start(norm_copy(i))
    n1 = nv[...]
    for i in range(len(around)):
        norm_copy(i).wait_recv()
        n1 = n1 + nq[i]
    nv2[...] = n1

    def norm_copy2(i):
        return remote(nv2, nq2.at[i], n2_s.at[i], n2_r.at[i], dev(x, y, z + i + 1, c))

    for i in range(7):
        out.start(norm_copy2(i))
    for i in range(7):
        norm_copy2(i).wait_recv()
        n1 = n1 + nq2[i]
    norm_sq = jnp.sum(n1, axis=1, keepdims=True)
    limit = math.sqrt(float(OWN * 256))
    clip = jnp.minimum(1.0, limit / (jnp.sqrt(norm_sq) + 1e-06))

    scaled = gsum * clip
    momentum = m_base + 0.1 * scaled
    variance = v_base + 0.05 * scaled * scaled
    update = momentum / first_fix / (jnp.sqrt(variance / second_fix) + 1e-08)
    fresh = kept - 0.0001 * update
    wg[rep] = fresh.astype(BF16)

    def along_z(i):
        zz = mod(zl + i, 4)
        return remote(wg.at[rep], wg.at[rep], w_s.at[i - 1], w_r.at[rep], dev(x, y, zh * 4 + zz, c))

    def along_y(i, j):
        slot = y * 4 + mod(zl + j, 4)
        return remote(wg.at[slot], wg.at[slot], w_s.at[3 + 3 * j + i - 1], w_r.at[slot], dev(x, y + i, z, c))

    def arrival(slot):
        remote(wg.at[slot], wg.at[slot], w_s.at[0], w_r.at[slot], dev(x, y + 1, z, c)).wait_recv()

    for i in range(1, 4):
        out.start(along_z(i))
    for i in range(1, 4):
        out.start(along_y(i, 0))

    def peak(v, a, b):
        return jnp.max(jnp.max(jnp.abs(v[a:b]), axis=0, keepdims=True), axis=1, keepdims=True)

    m_top = [peak(momentum, a, b) for a, b in SLOT_ROWS]
    v_top = [peak(variance, a, b) for a, b in SLOT_ROWS]
    for i, slot in ((0, 0), (1, 4)):
        ex[i] = jnp.concatenate(
            [jnp.broadcast_to(m_top[slot], (4, 128)), jnp.broadcast_to(v_top[slot], (4, 128))], axis=0
        )
    owner = shard * 16 + rep

    def edge_copy(i):
        other = mod(owner + (1 if i else -1), 256)
        return remote(ex.at[i], fx.at[1 - i], e_s.at[i], e_r.at[1 - i], (other // 16, other % 16))

    for i in (0, 1):
        out.start(edge_copy(i))
    nm_ref[...] = fresh
    up_ref[...] = update

    for j in (1, 3, 2):
        arrival(y * 4 + mod(zl + j, 4))
        for i in range(1, 4):
            out.start(along_y(i, j))

    for i in (0, 1):
        edge_copy(i).wait_recv()
    flat = jnp.full((1, 128), owner, jnp.int32)
    for slot, i, live in ((0, 0, flat > 0), (4, 1, flat < 255)):
        m_top[slot] = jnp.where(live, jnp.maximum(m_top[slot], fx[i, 0:1]), m_top[slot])
        v_top[slot] = jnp.where(live, jnp.maximum(v_top[slot], fx[i, 4:5]), v_top[slot])
    lane = lax.broadcasted_iota(jnp.int32, (1, 128), 1)
    m_row = jnp.zeros((1, 128), F32)
    v_row = jnp.zeros((1, 128), F32)
    for i, (a, b) in enumerate(SLOT_ROWS):
        mn_ref[a:b, :] = momentum[a:b] / (m_top[i] + 1e-06)
        vn_ref[a:b, :] = variance[a:b] / (v_top[i] + 1e-06)
        m_row = jnp.where(lane == i, m_top[i], m_row)
        v_row = jnp.where(lane == i, v_top[i], v_row)
    tb_ref[0:1, :] = m_row
    tb_ref[1:2, :] = v_row

    for i in range(1, 4):
        for j in range(4):
            arrival(mod(y + i, 4) * 4 + j)
    for i in range(16):
        wt_ref[i * ROWS : (i + 1) * ROWS, :] = wg[i]
    out.finish()


def on_device(grads, momentum_codes, variance_codes, momentum_scale, variance_scale, master, step):
    block = jax.ShapeDtypeStruct((ROWS, 128), F32)
    vmem = pl.BlockSpec(memory_space=pltpu.VMEM)
    smem = pl.BlockSpec(memory_space=pltpu.SMEM)
    sem = pltpu.SemaphoreType.DMA

    def f32(*shape):
        return pltpu.VMEM(shape + (128,), F32)

    new_master, weights, update, m_norm, v_norm, table = pl.pallas_call(
        kernel,
        out_shape=(
            block,
            jax.ShapeDtypeStruct((16 * ROWS, 128), BF16),
            block,
            block,
            block,
            jax.ShapeDtypeStruct((2, 128), F32),
        ),
        in_specs=[pl.BlockSpec(memory_space=pl.ANY), vmem, vmem, smem, smem, vmem, smem],
        out_specs=(vmem,) * 6,
        scratch_shapes=[
            pltpu.VMEM((1, 1, HALF), BF16),
            pltpu.VMEM((1, 1, HALF), BF16),
            f32(4, 2, 16, RA),
            f32(4, 2, 16, RB),
            f32(8, 2, 8, RC),
            f32(6, 16, RA),
            f32(6, 16, RB),
            f32(14, 8, RC),
            f32(4, 2, 4, RA),
            f32(4, 2, 4, RB),
            f32(4, 4, RC),
            f32(6, 4, RA),
            f32(6, 4, RB),
            f32(8, RA),
            f32(8, RB),
            f32(7, RA),
            f32(7, RB),
            f32(15, RC),
            f32(1),
            f32(31, 1),
            f32(1),
            f32(7, 1),
            f32(2, 8),
            f32(2, 8),
            pltpu.VMEM((16, ROWS, 128), BF16),
            sem((32,)),
        ]
        + [sem((n,)) for n in (32, 6, 6, 14, 6, 6, 7, 7, 15, 31, 7, 2) for _ in range(2)]
        + [sem((15,)), sem((16,))],
        compiler_params=pltpu.CompilerParams(
            collective_id=0, has_side_effects=True, vmem_limit_bytes=48 * 2**20
        ),
        name="adamw_step",
    )(
        grads,
        momentum_codes.reshape(ROWS, 128),
        variance_codes.reshape(ROWS, 128),
        momentum_scale,
        variance_scale,
        master.reshape(ROWS, 128),
        step,
    )
    return (
        new_master.reshape(-1),
        weights.reshape(-1),
        update.reshape(-1),
        m_norm.reshape(-1),
        v_norm.reshape(-1),
        table[0, :5],
        table[1, :5],
    )


def solution(mesh):
    own = P(("shard", "rep"))
    return jax.shard_map(
        on_device,
        mesh=mesh,
        in_specs=(P("shard", "rep", None), own, own, own, own, own, P()),
        out_specs=(own, P("shard"), own, own, own, own, own),
        check_vma=False,
    )
```

time: 718 us -> 69.3 us (0.10)
  waiting for transfers between devices: 552 us -> 0 us
  blocking collectives: 117 us -> 0 us
  Pallas kernels: 0 us -> 60.4 us
  other arithmetic: 20.1 us -> 0 us
  between operations: 17 us -> 1.3 us
    unnamed x4 -> x0, waiting for transfers between devices: 541 us -> none
    psum x1 -> x0, blocking collectives: 75.3 us -> none  [on_device(): norm_sq = lax.psum(jnp.sum(gsum * gsum), ('shard', 'rep'))]
    pallas_call x0 -> x1, Pallas kernels: none -> 60.4 us  [on_device(): pl.pallas_call(kernel, out_shape=(block, jax.ShapeDtypeStruct((16 * ROWS,...]
    all_gather x1 -> x0, blocking collectives: 41.7 us -> none  [on_device(): lax.all_gather(new_master.astype(jnp.bfloat16), 'rep', axis=0, tiled=True)]
    convert_element_type x2 -> x0, other arithmetic: 11.5 us -> none  [the longest x1 10.8 us: on_device(): grad_terms = grads.reshape(-1).astype(jnp.float32)]
    ppermute x2 -> x0, waiting for transfers between devices: 10.7 us -> none  [the longest x1 7.18 us: extended(): lax.ppermute(lax.slice_in_dim(block, block.shape[dim] - width, None, axis...]
  transfers between devices with their start and end apart: 4 -> 0, of which waited for: 4 -> 0; matrix products, arithmetic and copies ran while one was open for 0% -> 0% of each run, Pallas kernels for 0% -> 0%
where the time goes in v1:
time: 69.3 us; the launch traced here: 69 us
  Pallas kernels  60.4 us (87%)
  local copies, waits for them, and re-layouts  7.28 us (11%)
  between operations  1.3 us (2%)
    pallas_call x1, Pallas kernels, on_device(): pl.pallas_call(kernel, out_shape=(block, jax.ShapeDtypeStruct((16 * ROWS,...  60.4 us
    unnamed x15, local copies, waits for them, and re-layouts  6.76 us

profile of v1, /device:TPU:2, one launch (start us, length us, event | category | flops | bytes accessed | tf_op | source)
XLA Modules:
  0.0 69.0 jit_solution(5280318218795755720)
XLA Ops:
  1.3 0.0 copy-start
  1.3 0.7 %copy-done = s32[8192]{0:T(1024)S(1)} copy-done((s32[8192]{0:T(1024)S(1)}, s32[8192]{0:T(1024)}, u32[]{:S(2)}) %copy-start) | copy-done | bytes 32792
  2.0 0.0 copy-start.1
  2.0 0.8 %copy-done.1 = s32[8192]{0:T(1024)S(1)} copy-done((s32[8192]{0:T(1024)S(1)}, s32[8192]{0:T(1024)}, u32[]{:S(2)}) %copy-start.1) | copy-done | bytes 32792
  2.8 0.0 copy-start.2
  2.8 0.8 %copy-done.2 = f32[8192]{0:T(1024)S(1)} copy-done((f32[8192]{0:T(1024)S(1)}, f32[8192]{0:T(1024)}, u32[]{:S(2)}) %copy-start.2) | copy-done | bytes 32792
  3.6 0.0 copy-start.3
  3.6 0.7 copy-done.3
  4.2 0.0 copy-start.4
  4.2 0.7 copy-done.4
  4.9 60.4 %adamw_step.1 = (f32[64,128]{1,0:T(8,128)S(1)}, bf16[1024,128]{1,0:T(8,128)(2,1)S(1)}, f32[64,128]{1,0:T(8,128)S(1)}, f32[64,128]{1,0:T(8,128)S(1)}, f32[64,128]{1,0:T(8,128)S(1)}, /*index=5*/f32[2,128]{1,0:T(2,128)S(1)}) custom-call(bf16[1,1,2097152]{2,1,0:T(2,128)(2,1)} %g_ref.1, s32[64,128]{1,0:T(8,128)S(1)} %bitcast.13, s32[64,128]{1,0:T(8,128)S(1)} %bitcast.14, ...), custom_call_target="tpu_custom_call" | custom-call | tf_op jit(solution)/shard_map/adamw_step/pallas_call | solution.py:452
  65.3 0.5 slice_bitcast_fusion
  65.8 0.6 copy.20
  66.4 0.7 %copy.21 = bf16[131072]{0:T(1024)(128)(2,1)} copy(bf16[131072]{0:T(1024)(128)(2,1)S(1)} %bitcast.12) | data formatting | bytes 524288
  67.1 0.6 copy.22
  67.8 0.6 copy.23
  68.4 0.6 copy.24
Async XLA Ops:
  1.3 0.8 %copy-start = (s32[8192]{0:T(1024)S(1)}, s32[8192]{0:T(1024)}, u32[]{:S(2)}) copy-start(s32[8192]{0:T(1024)} %param.8) | copy-start | bytes 98308
  2.0 0.8 %copy-start.1 = (s32[8192]{0:T(1024)S(1)}, s32[8192]{0:T(1024)}, u32[]{:S(2)}) copy-start(s32[8192]{0:T(1024)} %param.9) | copy-start | bytes 98308
  2.8 0.8 %copy-start.2 = (f32[8192]{0:T(1024)S(1)}, f32[8192]{0:T(1024)}, u32[]{:S(2)}) copy-start(f32[8192]{0:T(1024)} %param.12) | copy-start | bytes 98308
  3.6 0.7 copy-start.3
  4.2 0.7 copy-start.4
